TPU v7x, 768 devices: a whole 4x8x12 slice. The times are simulated.
768 devices in a mesh: outer: 12 (over z), inner: 2 (over core), heads: 32 (over y, x).
Axes of the slice: x: 4, y: 8, z: 12, core: 2. Of those that a mesh axis runs over, the one named last changes fastest.
Arguments:
- lin_query: bfloat16 [3072, 8192], P(('outer', 'inner'), 'heads'), may hold values from -6 to 6
- lin_key: bfloat16 [3072, 8192], P(('outer', 'inner'), 'heads'), may hold values from -6 to 6
- lin_value: bfloat16 [3072, 8192], P(('outer', 'inner'), 'heads'), may hold values from -18 to 18
- gate_input: bfloat16 [3072, 8192], P(('outer', 'inner'), 'heads'), may hold values from -6 to 6
- norm_gain: bfloat16 [8192], P('heads'), may hold values from 0.099609375 to 1.8984375
- segment_ids: int32 [3072], P(('outer', 'inner')), may hold values from 0 to 15, never falling along the last dimension, each value on 1 to 384 neighbouring positions
- soft_query: bfloat16 [3072, 8192], P(('outer', 'inner'), 'heads'), may hold values from -10 to 10
- soft_key: bfloat16 [3072, 8192], P(('outer', 'inner'), 'heads'), may hold values from -4 to 4
Outputs:
- linear_out: bfloat16 [3072, 8192], P(('outer', 'inner'), 'heads')
- attended: bfloat16 [3072, 8192], P(('outer', 'inner'), 'heads')
Inputs may be any that keep to these rules, and one draw needn't show every extreme that they name: `segment_ids`: numbers never fall along the sequence, every number from 0 to 15 is used, and a document has at most 384 tokens.
All inputs are finite; a program needn't handle non-finite values.
Results may differ from a plain program's by a relative error of at most 0.0062.
Values may be sent and summed in bfloat16 or wider, within the bound.
A program may use at most 32 MiB of HBM per device.

v0:
```python
import math

import jax
import jax.numpy as jnp
from jax import lax
from jax.sharding import PartitionSpec as P

H = 64
DH = 128
SPAN = 3


def prefix(part, axis, combine, identity):
    place = lax.axis_index(axis)
    gathered = jax.tree.map(lambda a: lax.all_gather(a, axis), part)
    state = jax.tree.map(lambda a, e: jnp.zeros_like(a) + jnp.asarray(e, a.dtype), part, identity)

    def one(lap, state):
        return combine(
            state, jax.tree.map(lambda a: lax.dynamic_index_in_dim(a, lap, 0, False), gathered)
        )

    return lax.fori_loop(0, place, one, state)


def passed_along(shard, axis, by):
    length = lax.axis_size(axis)
    pairs = [(i, i + by) for i in range(length) if 0 <= i + by < length]
    return lax.ppermute(shard, axis, pairs)


def merge_states(earlier, later):
    joined_state = later[0] + jnp.where(earlier[1] == later[1], earlier[0], 0.0)
    empty_later = later[1] < 0
    return (
        jnp.where(empty_later, earlier[0], joined_state),
        jnp.where(empty_later, earlier[1], later[1]),
    )


def per_device(
    lin_query, lin_key, lin_value, gate_input, norm_gain, segment_ids, soft_query, soft_key
):
    tokens = lin_query.shape[0]
    columns = lin_query.shape[1]
    local_heads = columns // DH
    head_shape = (tokens, local_heads, DH)
    queries = lin_query.reshape(head_shape)
    key_rows = lin_key.reshape(head_shape)
    value_rows = lin_value.reshape(head_shape)
    position = lax.axis_index(("outer", "inner"))
    token_index = jnp.arange(tokens, dtype=jnp.int32)
    causal = token_index[:, None] >= token_index[None, :]
    same_doc = segment_ids[:, None] == segment_ids[None, :]
    raw_scores = jnp.einsum("thd,shd->hts", queries, key_rows, preferred_element_type=jnp.float32)
    intra_weights = jnp.where((causal & same_doc)[None], raw_scores, 0.0).astype(jnp.bfloat16)
    intra_part = jnp.einsum(
        "hts,shd->thd", intra_weights, value_rows, preferred_element_type=jnp.float32
    )
    final_doc = segment_ids[-1]
    kept = jnp.where(
        (segment_ids == final_doc)[:, None, None], key_rows, jnp.zeros((), jnp.bfloat16)
    )
    own_state = jnp.einsum("thd,the->hde", kept, value_rows, preferred_element_type=jnp.float32)
    identity = (jnp.zeros_like(own_state), jnp.array(-1, jnp.int32))
    group_states, group_docs = (
        lax.all_gather(own_state[None], "inner", axis=0, tiled=True),
        lax.all_gather(final_doc[None], "inner", axis=0, tiled=True),
    )
    group_width = lax.axis_size("inner")
    inner_place = lax.axis_index("inner")
    members = jnp.arange(group_width, dtype=jnp.int32)
    before_doc = jnp.sum(jnp.where(members == inner_place - 1, group_docs, 0))
    prefix_doc = jnp.where(inner_place > 0, before_doc, -1).astype(jnp.int32)
    prefix_weight = ((members < inner_place) & (group_docs == prefix_doc)).astype(jnp.float32)
    total_doc = group_docs[group_width - 1]
    total_weight = (group_docs == total_doc).astype(jnp.float32)
    prefix_state = jnp.einsum(
        "m,mhde->hde", prefix_weight, group_states, precision=lax.Precision.HIGHEST
    )
    total_state = jnp.einsum(
        "m,mhde->hde", total_weight, group_states, precision=lax.Precision.HIGHEST
    )
    group_before = prefix((total_state, total_doc), "outer", merge_states, identity)
    incoming = merge_states(group_before, (prefix_state, prefix_doc))
    carried_state, carried_doc = incoming
    carried_part = jnp.einsum(
        "thd,hde->the", queries.astype(jnp.float32), carried_state, precision=lax.Precision.HIGHEST
    )
    mixed = intra_part + jnp.where((segment_ids == carried_doc)[:, None, None], carried_part, 0.0)
    partial_squares = jnp.sum(mixed * mixed, axis=(1, 2))
    total_squares = lax.psum(partial_squares, "heads")
    inv_norm = lax.rsqrt(total_squares / (H * DH) + 1e-05)
    gain_cols = norm_gain.astype(jnp.float32).reshape(1, local_heads, DH)
    gate_cols = jax.nn.sigmoid(gate_input.astype(jnp.float32)).reshape(head_shape)
    linear_out = (
        (mixed * inv_norm[:, None, None] * gain_cols * gate_cols)
        .astype(jnp.bfloat16)
        .reshape(tokens, columns)
    )
    key_parts = []
    value_parts = []
    doc_parts = []
    pos_parts = []
    for back_steps in range(SPAN, 0, -1):
        got_keys, got_values, got_docs = passed_along(
            (soft_key, linear_out, segment_ids), ("outer", "inner"), back_steps
        )
        key_parts.append(got_keys)
        value_parts.append(got_values)
        doc_parts.append(got_docs)
        pos_parts.append((position - back_steps) * tokens + token_index)
    key_parts.append(soft_key)
    value_parts.append(linear_out)
    doc_parts.append(segment_ids)
    pos_parts.append(position * tokens + token_index)
    window_keys = jnp.concatenate(key_parts, axis=0).reshape(-1, local_heads, DH)
    window_values = jnp.concatenate(value_parts, axis=0).reshape(-1, local_heads, DH)
    window_docs = jnp.concatenate(doc_parts, axis=0)
    window_pos = jnp.concatenate(pos_parts, axis=0)
    query_pos = position * tokens + token_index
    scores = jnp.einsum(
        "thd,shd->hts",
        soft_query.reshape(head_shape),
        window_keys,
        preferred_element_type=jnp.float32,
    ) * (1.0 / math.sqrt(DH))
    visible = (
        (segment_ids[:, None] == window_docs[None, :])
        & (window_pos[None, :] <= query_pos[:, None])
        & (window_pos >= 0)[None, :]
    )
    masked = jnp.where(visible[None], scores, -jnp.inf)
    row_top = jnp.max(masked, axis=2, keepdims=True)
    exponent = jnp.where(visible[None], jnp.exp(masked - row_top), 0.0)
    soft_weights = (exponent / jnp.sum(exponent, axis=2, keepdims=True)).astype(jnp.bfloat16)
    attended = jnp.einsum(
        "hts,shd->thd", soft_weights, window_values, preferred_element_type=jnp.float32
    )
    return (linear_out, attended.astype(jnp.bfloat16).reshape(tokens, columns))


def solution(mesh):
    return jax.shard_map(
        per_device,
        mesh=mesh,
        in_specs=(
            P(("outer", "inner"), "heads"),
            P(("outer", "inner"), "heads"),
            P(("outer", "inner"), "heads"),
            P(("outer", "inner"), "heads"),
            P("heads"),
            P(("outer", "inner")),
            P(("outer", "inner"), "heads"),
            P(("outer", "inner"), "heads"),
        ),
        out_specs=(P(("outer", "inner"), "heads"), P(("outer", "inner"), "heads")),
        check_vma=False,
    )
```

profile of v0, /device:TPU:576, one launch (start us, length us, event | category | flops | bytes accessed | tf_op | source)
XLA Modules:
  0.0 212.3 jit_solution(10032687193947956614)
XLA Ops:
  7.3 1.3 dynamic-slice
  8.6 1.9 fusion.64
  10.5 1.8 all-reduce
  12.3 1.3 dynamic-slice.1
  13.5 1.3 broadcast_compare_fusion.2
  14.8 0.9 copy.60
  15.8 1.0 fusion.27
  16.8 2.0 all-gather
  18.8 1.2 fusion.63
  20.0 2.0 fusion.19
  22.0 3.2 %collective-permute-start.3 = (s32[128]{0:T(128)}, s32[128]{0:T(128)S(1)}, u32[]{:S(2)}, u32[]{:S(2)}) collective-permute-start(s32[128]{0:T(128)} %param.15), channel_id=1, source_target_pairs={{0,96},{32,128},{64,160},{96,192},{128,224},{160,256},{192,288},{2... | collective-permute-start | bytes 1544 | tf_op jit(solution)/shard_map/ppermute | solution.py:29
  25.2 3.4 %collective-permute-start.4 = (s32[128]{0:T(128)}, s32[128]{0:T(128)S(1)}, u32[]{:S(2)}, u32[]{:S(2)}) collective-permute-start(s32[128]{0:T(128)} %param.15), channel_id=1, source_target_pairs={{0,64},{32,96},{64,128},{96,160},{128,192},{160,224},{192,256},{22... | collective-permute-start | bytes 1544 | tf_op jit(solution)/shard_map/ppermute | solution.py:29
  28.6 1.9 collective-permute-start.5
  30.5 1.0 copy.43
  31.5 1.9 collective-permute-start.6
  33.4 1.9 collective-permute-start.7
  35.4 0.6 fusion.50
  36.9 0.7 fusion.17
  37.6 24.3 %all-reduce.1 = s32[12]{0:T(128)S(1)} all-reduce(s32[12]{0:T(128)S(1)} %get-tuple-element.59), channel_id=1, replica_groups=mesh['outer'=12,'inner'=2,'heads'=32] {'outer'}, use_global_device_ids=true, to_apply=%add.1 | all-reduce | flops 12 | bytes 96
  62.0 1.9 collective-permute-start.8
  64.3 3.6 %collective-permute-done.8 = bf16[128,256]{0,1:T(8,128)(2,1)S(1)} collective-permute-done((bf16[128,256]{0,1:T(8,128)(2,1)S(1)}, bf16[128,256]{0,1:T(8,128)(2,1)S(1)}, u32[]{:S(2)}, u32[]{:S(2)}) %collective-permute-start.8) | collective-permute-done | bytes 65568 | tf_op jit(solution)/shard_map/ppermute | solution.py:29
  68.3 10.5 %all-gather.4.cloned.1.call-done = f32[24,128,128]{2,1,0:T(8,128)} async-done(((f32[2,128,128]{2,1,0:T(8,128)}), f32[24,128,128]{2,1,0:T(8,128)}) %all-gather.4.cloned.1.call-update) | async-done | bytes 1572880 | tf_op jit(solution)/shard_map/all_gather | solution.py:15
  78.8 32.1 %while.12 = (s32[]{:T(128)}, f32[2,128,128]{2,1,0:T(8,128)S(1)}, s32[]{:T(128)}, s32[]{:T(128)}, s32[12]{0:T(128)S(1)}, /*index=5*/f32[12,2,128,128]{3,2,1,0:T(8,128)}, s32[]{:T(128)}, s32[]{:T(128)}, s32[]{:T(128)}) while((s32[]{:T(128)}, f32[2,128,128]{2,1,0:T(8,128)S(1)}, s32[]{:T(128)}, s32[]{:T(128)}, s32[12]{0:T(128)S(1)}, ...), condition=%wide.region_2.3_spmd, body=%wide.region_1.2_spmd.sunk | while | flops 98312 | bytes 393392 | solution.py:23
  78.8 0.7 dynamic_slice.12
  80.7 1.0 fusion.81
  82.4 0.7 dynamic_slice.12
  84.3 1.0 fusion.81
  85.9 0.7 dynamic_slice.12
  87.9 1.0 fusion.81
  89.5 0.7 dynamic_slice.12
  91.4 1.0 fusion.81
  93.0 0.7 dynamic_slice.12
  95.0 1.0 fusion.81
  96.6 0.7 dynamic_slice.12
  98.5 1.0 fusion.81
  100.2 0.7 dynamic_slice.12
  102.1 1.0 fusion.81
  103.7 0.7 dynamic_slice.12
  105.7 1.0 fusion.81
  107.3 0.7 dynamic_slice.12
  109.2 1.0 fusion.81
  111.5 74.2 %psum.7 = f32[128]{0:T(128)S(1)} all-reduce(f32[128]{0:T(128)S(1)} %get-tuple-element.62), channel_id=1, replica_groups=mesh['outer'=12,'inner'=2,'heads'=32] {'heads'}, use_global_device_ids=true, to_apply=%region_4.5 | all-reduce | flops 128 | bytes 1024 | tf_op jit(solution)/shard_map/psum | solution.py:92
  185.9 1.9 collective-permute-start
  187.8 7.2 %collective-permute-start.1 = (bf16[128,256]{0,1:T(8,128)(2,1)S(1)}, bf16[128,256]{0,1:T(8,128)(2,1)S(1)}, u32[]{:S(2)}, u32[]{:S(2)}) collective-permute-start(bf16[128,256]{0,1:T(8,128)(2,1)S(1)} %bitcast.112), channel_id=1, source_target_pairs={{0,64},{32,96},{64,128},{96,160},{128,192},{160,224},{192,256},{22... | collective-permute-start | bytes 196616 | tf_op jit(solution)/shard_map/ppermute | solution.py:29
  195.0 6.1 %collective-permute-start.2 = (bf16[128,256]{0,1:T(8,128)(2,1)S(1)}, bf16[128,256]{0,1:T(8,128)(2,1)S(1)}, u32[]{:S(2)}, u32[]{:S(2)}) collective-permute-start(bf16[128,256]{0,1:T(8,128)(2,1)S(1)} %bitcast.113), channel_id=1, source_target_pairs={{0,32},{32,64},{64,96},{96,128},{128,160},{160,192},{192,224},{224... | collective-permute-start | bytes 196616 | tf_op jit(solution)/shard_map/ppermute | solution.py:29
  201.5 0.7 copy.50
  202.2 2.1 collective-permute-done.2
  204.7 0.7 copy.51
  (43 shorter events, 2.5 us)
Async XLA Ops:
  7.2 60.8 %copy-start = (bf16[128,256]{1,0:T(8,128)(2,1)S(1)}, bf16[128,256]{1,0:T(8,128)(2,1)}, u32[]{:S(2)}) copy-start(bf16[128,256]{1,0:T(8,128)(2,1)} %param.16) | copy-start | bytes 196612
  7.2 29.5 %copy-start.4 = (s32[128]{0:T(128)S(1)}, s32[128]{0:T(128)}, u32[]{:S(2)}) copy-start(s32[128]{0:T(128)} %param.15) | copy-start | bytes 1540
  7.2 29.5 %copy-start.5 = (bf16[256]{0:T(256)(128)(2,1)S(1)}, bf16[256]{0:T(256)(128)(2,1)}, u32[]{:S(2)}) copy-start(bf16[256]{0:T(256)(128)(2,1)} %param.14) | copy-start | bytes 1540
  7.2 29.6 %copy-start.3 = (bf16[128,256]{1,0:T(8,128)(2,1)S(1)}, bf16[128,256]{1,0:T(8,128)(2,1)}, u32[]{:S(2)}) copy-start(bf16[128,256]{1,0:T(8,128)(2,1)} %param.13) | copy-start | bytes 196612
  7.2 71.5 %all-gather.4.cloned.1.call-start = ((), (), s32[]{:S(2)}) async-start(), calls=%async_computation | async-start | bytes 1703936 | tf_op jit(solution)/shard_map/all_gather | solution.py:15
  22.0 40.0 %collective-permute-start.3 = (s32[128]{0:T(128)}, s32[128]{0:T(128)S(1)}, u32[]{:S(2)}, u32[]{:S(2)}) collective-permute-start(s32[128]{0:T(128)} %param.15), channel_id=1, source_target_pairs={{0,96},{32,128},{64,160},{96,192},{128,224},{160,256},{192,288},{2... | collective-permute-start | bytes 1544 | tf_op jit(solution)/shard_map/ppermute | solution.py:29
  25.2 38.8 %collective-permute-start.4 = (s32[128]{0:T(128)}, s32[128]{0:T(128)S(1)}, u32[]{:S(2)}, u32[]{:S(2)}) collective-permute-start(s32[128]{0:T(128)} %param.15), channel_id=1, source_target_pairs={{0,64},{32,96},{64,128},{96,160},{128,192},{160,224},{192,256},{22... | collective-permute-start | bytes 1544 | tf_op jit(solution)/shard_map/ppermute | solution.py:29
  28.6 35.4 %collective-permute-start.5 = (s32[128]{0:T(128)}, s32[128]{0:T(128)S(1)}, u32[]{:S(2)}, u32[]{:S(2)}) collective-permute-start(s32[128]{0:T(128)} %param.15), channel_id=1, source_target_pairs={{0,32},{32,64},{64,96},{96,128},{128,160},{160,192},{192,224},{224... | collective-permute-start | bytes 1544 | tf_op jit(solution)/shard_map/ppermute | solution.py:29
  31.5 32.8 %collective-permute-start.6 = (bf16[128,256]{0,1:T(8,128)(2,1)S(1)}, bf16[128,256]{0,1:T(8,128)(2,1)S(1)}, u32[]{:S(2)}, u32[]{:S(2)}) collective-permute-start(bf16[128,256]{0,1:T(8,128)(2,1)S(1)} %copy.43), channel_id=1, source_target_pairs={{0,96},{32,128},{64,160},{96,192},{128,224},{160,256},{192,288},{2... | collective-permute-start | bytes 196616 | tf_op jit(solution)/shard_map/ppermute | solution.py:29
  33.4 30.9 %collective-permute-start.7 = (bf16[128,256]{0,1:T(8,128)(2,1)S(1)}, bf16[128,256]{0,1:T(8,128)(2,1)S(1)}, u32[]{:S(2)}, u32[]{:S(2)}) collective-permute-start(bf16[128,256]{0,1:T(8,128)(2,1)S(1)} %copy.43), channel_id=1, source_target_pairs={{0,64},{32,96},{64,128},{96,160},{128,192},{160,224},{192,256},{22... | collective-permute-start | bytes 196616 | tf_op jit(solution)/shard_map/ppermute | solution.py:29
  62.0 5.9 %collective-permute-start.8 = (bf16[128,256]{0,1:T(8,128)(2,1)S(1)}, bf16[128,256]{0,1:T(8,128)(2,1)S(1)}, u32[]{:S(2)}, u32[]{:S(2)}) collective-permute-start(bf16[128,256]{0,1:T(8,128)(2,1)S(1)} %copy.43), channel_id=1, source_target_pairs={{0,32},{32,64},{64,96},{96,128},{128,160},{160,192},{192,224},{224... | collective-permute-start | bytes 196616 | tf_op jit(solution)/shard_map/ppermute | solution.py:29
  68.0 42.9 %copy-start.2 = (bf16[128,256]{1,0:T(8,128)(2,1)S(1)}, bf16[128,256]{1,0:T(8,128)(2,1)}, u32[]{:S(2)}) copy-start(bf16[128,256]{1,0:T(8,128)(2,1)} %param.10) | copy-start | bytes 196612
  68.2 42.9 %copy-start.1 = (bf16[128,256]{1,0:T(8,128)(2,1)S(1)}, bf16[128,256]{1,0:T(8,128)(2,1)}, u32[]{:S(2)}) copy-start(bf16[128,256]{1,0:T(8,128)(2,1)} %param.12) | copy-start | bytes 196612
  185.9 16.3 %collective-permute-start = (bf16[128,256]{0,1:T(8,128)(2,1)S(1)}, bf16[128,256]{0,1:T(8,128)(2,1)S(1)}, u32[]{:S(2)}, u32[]{:S(2)}) collective-permute-start(bf16[128,256]{0,1:T(8,128)(2,1)S(1)} %bitcast.111), channel_id=1, source_target_pairs={{0,96},{32,128},{64,160},{96,192},{128,224},{160,256},{192,288},{2... | collective-permute-start | bytes 196616 | tf_op jit(solution)/shard_map/ppermute | solution.py:29
  187.8 14.4 %collective-permute-start.1 = (bf16[128,256]{0,1:T(8,128)(2,1)S(1)}, bf16[128,256]{0,1:T(8,128)(2,1)S(1)}, u32[]{:S(2)}, u32[]{:S(2)}) collective-permute-start(bf16[128,256]{0,1:T(8,128)(2,1)S(1)} %bitcast.112), channel_id=1, source_target_pairs={{0,64},{32,96},{64,128},{96,160},{128,192},{160,224},{192,256},{22... | collective-permute-start | bytes 196616 | tf_op jit(solution)/shard_map/ppermute | solution.py:29
  195.0 9.3 %collective-permute-start.2 = (bf16[128,256]{0,1:T(8,128)(2,1)S(1)}, bf16[128,256]{0,1:T(8,128)(2,1)S(1)}, u32[]{:S(2)}, u32[]{:S(2)}) collective-permute-start(bf16[128,256]{0,1:T(8,128)(2,1)S(1)} %bitcast.113), channel_id=1, source_target_pairs={{0,32},{32,64},{64,96},{96,128},{128,160},{160,192},{192,224},{224... | collective-permute-start | bytes 196616 | tf_op jit(solution)/shard_map/ppermute | solution.py:29
Sparse Core Ops, SparseCore 0:
  22.2 56.5 all-gather.3
where the time goes:
time: 213 us; the launch traced here: 212 us
  blocking collectives  102 us (48%)
  starting transfers between devices  29.4 us (14%)
  loops' own time  17.6 us (8%)
  waiting for transfers between devices  16.2 us (8%)
  local copies, waits for them, and re-layouts  15.1 us (7%)
  between operations  15.1 us (7%)
  other arithmetic  11.1 us (5%)
  matrix products  5.39 us (3%)
    psum x1, blocking collectives, per_device(): total_squares = lax.psum(partial_squares, 'heads')  74.2 us
    ppermute x9, starting transfers between devices, passed_along(): return lax.ppermute(shard, axis, pairs)  29.4 us
    unnamed x2, blocking collectives  26.2 us
    another operation x1, loops' own time, prefix(): return lax.fori_loop(0, place, one, state)  17.6 us
    all_gather x1, waiting for transfers between devices, prefix(): gathered = jax.tree.map(lambda a: lax.all_gather(a, axis), part)  10.5 us
    select_n x9, other arithmetic, merge_states(): jnp.where(empty_later, earlier[0], joined_state)  8.6 us
    dynamic_slice x9, local copies, waits for them, and re-layouts, one(): lax.dynamic_index_in_dim(a, lap, 0, False)  5.9 us
    ppermute x9, waiting for transfers between devices, passed_along(): return lax.ppermute(shard, axis, pairs)  5.7 us
  transfers between devices with their start and end apart: 10, of which 3 were waited for; matrix products, arithmetic and copies ran while one was open for 2% of the time, Pallas kernels for 0%

commit v1 on v0

v1 whole, which is shorter than its diff:
```python
import functools
import math

import jax
import jax.numpy as jnp
from jax import lax
from jax.experimental import pallas as pl
from jax.experimental.pallas import tpu as pltpu
from jax.sharding import PartitionSpec as P

DH = 128
X_CHIPS = 4
REACH = 3
MESH = pl.DeviceIdType.MESH
F32 = jnp.float32
BF16 = jnp.bfloat16


def matmul(a, b):
    return jnp.dot(a, b, preferred_element_type=F32)


def matmul_nt(a, b):
    return lax.dot_general(a, b, (((1,), (1,)), ((), ())), preferred_element_type=F32)


def matmul_tn(a, b):
    return lax.dot_general(a, b, (((0,), (0,)), ((), ())), preferred_element_type=F32)


def column(row):
    n = row.shape[1]
    return jnp.transpose(jnp.broadcast_to(row, (n, n)))


def kernel(
    groups, x_chips, y_chips, total_columns,
    q_in, k_in, v_in, g_in, gain_in, seg_in, sq_in, sk_in,
    lin_out, att_out,
    q, k, v, g, gain, seg, sq, sk,
    docs, state, states, keys, mid, mids, own_row, rows_y, rows_x,
    gates, mixed, weights,
    load_sem, doc_send, doc_recv, state_send, state_recv, key_send, key_recv, mid_send, mid_recv,
    y_send, y_recv, x_send, x_recv,
):
    z = lax.axis_index("outer")
    c = lax.axis_index("inner")
    h = lax.axis_index("heads")
    y, x = h // x_chips, h % x_chips
    tokens = q.shape[0]
    heads = q.shape[1] // DH

    def at(dz, core, head):
        return (lax.rem(z + dz + groups, groups), core, head)

    def later(j):
        n = c + j + 2 * groups
        return lax.rem(z + n // 2, groups), n % 2

    loads = [
        pltpu.make_async_copy(a, b, load_sem.at[i])
        for i, (a, b) in enumerate(
            ((seg_in, seg), (k_in, k), (v_in, v), (q_in, q), (gain_in, gain), (g_in, g), (sk_in, sk), (sq_in, sq))
        )
    ]
    for copy in loads:
        copy.start()

    barrier = pltpu.get_barrier_semaphore()

    def greet(device):
        pl.semaphore_signal(barrier, inc=1, device_id=device, device_id_type=MESH)

    other = (z, 1 - c, h)
    greet(other)
    for d in range(1, y_chips):
        greet((z, c, lax.rem(y + d, y_chips) * x_chips + x))
    for j in range(REACH + 1):
        for d in range(x_chips):
            if j or d:
                bz, bc = later(-j)
                greet((bz, bc, y * x_chips + lax.rem(x + d, x_chips)))

    for copy in loads[:3]:
        copy.wait()
    doc_row = seg[...].astype(F32)
    doc_col = column(doc_row)
    kept = doc_col == doc_row[:, tokens - 1 :]
    for i in range(heads):
        cols = slice(i * DH, (i + 1) * DH)
        masked = jnp.where(kept, k[:, cols].astype(F32), 0.0).astype(BF16)
        state[cols, :] = matmul_tn(masked, v[:, cols]).astype(BF16)

    pl.semaphore_wait(barrier, y_chips - 1 + (REACH + 1) * x_chips)

    near = at(c, 1 - c, h)
    far = at(1 + c, 1 - c, h)
    relay_slot = 2 * c

    def send(src, dst, dst_slot, sends, sent, recvs, device):
        copy = pltpu.make_async_remote_copy(
            src_ref=src,
            dst_ref=dst.at[dst_slot],
            send_sem=sends.at[sent],
            recv_sem=recvs.at[dst_slot],
            device_id=device,
            device_id_type=MESH,
        )
        copy.start()
        return copy

    def arrived(dst, slot, recvs):
        pltpu.make_async_copy(dst.at[slot], dst.at[slot], recvs.at[slot]).wait()

    sent = []
    for j in range(REACH):
        bz, bc = later(j + 1)
        sent.append(send(seg, docs, j, doc_send, j, doc_recv, (bz, bc, h)))

    def spread(src, dst, sends, recvs):
        sent.append(send(src, dst, 0, sends, 0, recvs, near))
        sent.append(send(src, dst, 2, sends, 1, recvs, far))

    def relay(dst, sends, recvs):
        sent.append(send(dst.at[relay_slot], dst, 1, sends, 2, recvs, other))

    spread(state, states, state_send, state_recv)
    loads[6].wait()
    spread(sk, keys, key_send, key_recv)

    loads[3].wait()
    at_t = lax.broadcasted_iota(jnp.int32, (tokens, tokens), 0)
    at_s = lax.broadcasted_iota(jnp.int32, (tokens, tokens), 1)
    own_seen = (at_t >= at_s) & (doc_col == doc_row)
    for i in range(heads):
        cols = slice(i * DH, (i + 1) * DH)
        intra = jnp.where(own_seen, matmul_nt(q[:, cols], k[:, cols]), 0.0).astype(BF16)
        mixed[:, cols] = matmul(intra, v[:, cols])
    loads[4].wait()
    loads[5].wait()
    gates[...] = jax.nn.sigmoid(g[...].astype(F32)) * gain[...].astype(F32)

    for j in range(REACH):
        arrived(docs, j, doc_recv)

    arrived(states, relay_slot, state_recv)
    relay(states, state_send, state_recv)
    arrived(states, 2 - relay_slot, state_recv)
    arrived(states, 1, state_recv)
    for i in range(heads):
        cols = slice(i * DH, (i + 1) * DH)
        q_f32 = q[:, cols].astype(F32)
        carried = None
        for j in range(REACH):
            last = docs[j].astype(F32)[:, tokens - 1 :]
            part = matmul(jnp.where(doc_col == last, q_f32, 0.0).astype(BF16), states[j, cols, :])
            carried = part if carried is None else carried + part
        mixed[:, cols] += carried

    square = mixed[...] * mixed[...]
    own_row[...] = matmul_nt(jnp.ones((8, heads * DH), BF16), square.astype(BF16))[:1]

    for d in range(1, y_chips):
        copy = pltpu.make_async_remote_copy(
            src_ref=own_row,
            dst_ref=rows_y.at[y],
            send_sem=y_send,
            recv_sem=y_recv,
            device_id=(z, c, lax.rem(y + d, y_chips) * x_chips + x),
            device_id_type=MESH,
        )
        copy.start()
    rows_y[y] = own_row[...]
    mid[...] = (mixed[...] * gates[...]).astype(BF16)
    spread(mid, mids, mid_send, mid_recv)

    loads[7].wait()
    arrived(keys, relay_slot, key_recv)
    relay(keys, key_send, key_recv)
    arrived(keys, 2 - relay_slot, key_recv)
    arrived(keys, 1, key_recv)
    scale = 1.0 / math.sqrt(DH)
    for i in range(heads):
        cols = slice(i * DH, (i + 1) * DH)
        query = sq[:, cols]
        parts = [jnp.where(own_seen, matmul_nt(query, sk[:, cols]) * scale, -jnp.inf)]
        for j in range(REACH):
            seen = doc_col == docs[j].astype(F32)
            parts.append(jnp.where(seen, matmul_nt(query, keys[j, :, cols]) * scale, -jnp.inf))
        top = parts[0]
        for part in parts[1:]:
            top = jnp.maximum(top, part)
        top = jnp.max(top, axis=1, keepdims=True)
        parts = [jnp.exp(part - top) for part in parts]
        total = jnp.sum(parts[0] + parts[1] + parts[2] + parts[3], axis=1, keepdims=True)
        for j, part in enumerate(parts):
            weights[i, j] = part / total

    if y_chips > 1:
        span = pl.ds(0, y_chips - 1)
        pltpu.make_async_copy(rows_y.at[span], rows_y.at[span], y_recv).wait()
    own_row2 = rows_x.at[0, x]
    own_row2[...] = jnp.sum(rows_y[...], axis=0)
    for j in range(REACH + 1):
        for d in range(x_chips):
            if j or d:
                bz, bc = later(j)
                copy = pltpu.make_async_remote_copy(
                    src_ref=own_row2,
                    dst_ref=rows_x.at[j, x],
                    send_sem=x_send,
                    recv_sem=x_recv.at[j],
                    device_id=(bz, bc, y * x_chips + lax.rem(x + d, x_chips)),
                    device_id_type=MESH,
                )
                copy.start()

    arrived(mids, relay_slot, mid_recv)
    relay(mids, mid_send, mid_recv)

    def inverse_norm(j):
        span = pl.ds(0, x_chips if j else x_chips - 1)
        pltpu.make_async_copy(rows_x.at[j, span], rows_x.at[j, span], x_recv.at[j]).wait()
        return lax.rsqrt(jnp.sum(rows_x[j], axis=0) / total_columns + 1e-05)

    inverse = inverse_norm(0)
    inverse_col = column(inverse)
    for i in range(heads):
        cols = slice(i * DH, (i + 1) * DH)
        lin_out[:, cols] = (mixed[:, cols] * gates[:, cols] * inverse_col).astype(BF16)

    arrived(mids, 2 - relay_slot, mid_recv)
    arrived(mids, 1, mid_recv)
    inverses = [inverse] + [inverse_norm(j + 1) for j in range(REACH)]
    for i in range(heads):
        cols = slice(i * DH, (i + 1) * DH)
        result = matmul((weights[i, 0] * inverses[0]).astype(BF16), mid[:, cols])
        for j in range(REACH):
            result += matmul((weights[i, j + 1] * inverses[j + 1]).astype(BF16), mids[j, :, cols])
        att_out[:, cols] = result.astype(BF16)

    for copy in sent:
        copy.wait_send()
    if y_chips > 1:
        span = pl.ds(0, y_chips - 1)
        pltpu.make_async_copy(rows_y.at[span], rows_y.at[span], y_send).wait()
    count = (REACH + 1) * x_chips - 1
    pltpu.make_async_copy(weights.at[0, 0, pl.ds(0, count)], weights.at[0, 0, pl.ds(0, count)], x_send).wait()


def per_device(mesh, *args):
    q, k, v, g, gain, seg, sq, sk = args
    tokens, columns = q.shape
    groups = mesh.shape["outer"]
    x_chips = min(X_CHIPS, mesh.shape["heads"])
    y_chips = mesh.shape["heads"] // x_chips
    total_columns = columns * mesh.shape["heads"]
    seg = seg.reshape(1, tokens)
    gain = gain.reshape(1, columns)
    dma = pltpu.SemaphoreType.DMA
    block = (tokens, columns)
    stacked = (columns, DH)
    return pl.pallas_call(
        functools.partial(kernel, groups, x_chips, y_chips, total_columns),
        out_shape=(jax.ShapeDtypeStruct(block, BF16), jax.ShapeDtypeStruct(block, BF16)),
        in_specs=[pl.BlockSpec(memory_space=pl.ANY)] * 8,
        out_specs=(pl.BlockSpec(memory_space=pltpu.VMEM), pl.BlockSpec(memory_space=pltpu.VMEM)),
        scratch_shapes=[
            pltpu.VMEM(block, BF16), pltpu.VMEM(block, BF16), pltpu.VMEM(block, BF16), pltpu.VMEM(block, BF16),
            pltpu.VMEM((1, columns), BF16), pltpu.VMEM((1, tokens), jnp.int32),
            pltpu.VMEM(block, BF16), pltpu.VMEM(block, BF16),
            pltpu.VMEM((REACH, 1, tokens), jnp.int32),
            pltpu.VMEM(stacked, BF16), pltpu.VMEM((REACH,) + stacked, BF16),
            pltpu.VMEM((REACH,) + block, BF16),
            pltpu.VMEM(block, BF16), pltpu.VMEM((REACH,) + block, BF16),
            pltpu.VMEM((1, tokens), F32),
            pltpu.VMEM((y_chips, 1, tokens), F32),
            pltpu.VMEM((REACH + 1, x_chips, 1, tokens), F32),
            pltpu.VMEM(block, F32), pltpu.VMEM(block, F32),
            pltpu.VMEM((columns // DH, REACH + 1, tokens, tokens), F32),
            dma((8,)),
            dma((REACH,)), dma((REACH,)), dma((3,)), dma((REACH,)), dma((3,)), dma((REACH,)), dma((3,)), dma((REACH,)),
            dma, dma, dma, dma((REACH + 1,)),
        ],
        compiler_params=pltpu.CompilerParams(collective_id=0, has_side_effects=True),
    )(q, k, v, g, gain, seg, sq, sk)


def solution(mesh):
    block = P(("outer", "inner"), "heads")
    return jax.shard_map(
        functools.partial(per_device, mesh),
        mesh=mesh,
        in_specs=(block, block, block, block, P("heads"), P(("outer", "inner")), block, block),
        out_specs=(block, block),
        check_vma=False,
    )
```

time: 213 us -> 39.6 us (0.19)
  the two profiles are of different devices: /device:TPU:576 before, /device:TPU:1 now
where the time goes in v1:
time: 39.6 us; the launch traced here: 39.3 us
  Pallas kernels  35.3 us (89%)
  local copies, waits for them, and re-layouts  3.35 us (8%)
  between operations  0.66 us (2%)
    pallas_call x1, Pallas kernels, per_device(): pl.pallas_call(functools.partial(kernel, groups, x_chips, y_chips, total_...  35.3 us
    unnamed x6, local copies, waits for them, and re-layouts  2.79 us

profile of v1, /device:TPU:1, one launch (start us, length us, event | category | flops | bytes accessed | tf_op | source)
XLA Modules:
  0.0 39.3 jit_solution(9399471036839868052)
XLA Ops:
  0.6 0.0 copy-start.1
  0.6 0.6 %copy-done.1 = bf16[256]{0:T(256)(128)(2,1)S(1)} copy-done((bf16[256]{0:T(256)(128)(2,1)S(1)}, bf16[256]{0:T(256)(128)(2,1)}, u32[]{:S(2)}) %copy-start.1) | copy-done | bytes 536
  1.3 0.6 %reshape.10.gain_in = bf16[1,256]{1,0:T(2,128)(2,1)} reshape(bf16[256]{0:T(256)(128)(2,1)S(1)} %copy-done.1) | data formatting | bytes 1024 | tf_op jit(solution)/shard_map/reshape | solution.py:259
  1.9 35.3 %shard_map.95 = (bf16[128,256]{1,0:T(8,128)(2,1)}, bf16[128,256]{1,0:T(8,128)(2,1)}) custom-call(bf16[128,256]{1,0:T(8,128)(2,1)} %q_in.1, bf16[128,256]{1,0:T(8,128)(2,1)} %k_in.1, bf16[128,256]{1,0:T(8,128)(2,1)} %v_in.1, bf16[128,256]{1,0:T(8,128)(2,1)} %g_in.1, bf16[1,256]{1,0:T(2,128)(2,1)} %reshape.10.gain_in, s32[1,128]{1,0:T(1,128)} %bitcast.1, ...), custom_call_target="tpu_custom_call" | custom-call | tf_op jit(solution)/shard_map/pallas_call | solution.py:263
  37.2 0.0 copy-start
  37.2 1.5 %copy.12 = bf16[128,256]{1,0:T(8,128)(2,1)} copy(bf16[128,256]{1,0:T(8,128)(2,1)} %get-tuple-element.4) | data formatting | bytes 131072
  38.7 0.0 copy-done
  38.7 0.6 %copy.13 = bf16[128,256]{1,0:T(8,128)(2,1)} copy(bf16[128,256]{1,0:T(8,128)(2,1)S(1)} %copy-done) | data formatting | bytes 131072
Async XLA Ops:
  0.6 0.7 %copy-start.1 = (bf16[256]{0:T(256)(128)(2,1)S(1)}, bf16[256]{0:T(256)(128)(2,1)}, u32[]{:S(2)}) copy-start(bf16[256]{0:T(256)(128)(2,1)} %param.12) | copy-start | bytes 1540
  37.2 1.5 %copy-start = (bf16[128,256]{1,0:T(8,128)(2,1)S(1)}, bf16[128,256]{1,0:T(8,128)(2,1)}, u32[]{:S(2)}) copy-start(bf16[128,256]{1,0:T(8,128)(2,1)} %get-tuple-element.5) | copy-start | bytes 196612

commit v2 on v1

v2 whole, which is shorter than its diff:
```python
import functools
import math

import jax
import jax.numpy as jnp
from jax import lax
from jax.experimental import pallas as pl
from jax.experimental.pallas import tpu as pltpu
from jax.sharding import PartitionSpec as P

DH = 128
X_CHIPS = 4
REACH = 3
MESH = pl.DeviceIdType.MESH
F32 = jnp.float32
BF16 = jnp.bfloat16


def matmul(a, b):
    return jnp.dot(a, b, preferred_element_type=F32)


def matmul_nt(a, b):
    return lax.dot_general(a, b, (((1,), (1,)), ((), ())), preferred_element_type=F32)


def matmul_tn(a, b):
    return lax.dot_general(a, b, (((0,), (0,)), ((), ())), preferred_element_type=F32)


def column(row):
    n = row.shape[1]
    return jnp.transpose(jnp.broadcast_to(row, (n, n)))


def kernel(
    groups, x_chips, y_chips, total_columns,
    q_in, k_in, v_in, g_in, gain_in, seg_in, sq_in, sk_in,
    lin_out, att_out,
    q, k, v, g, gain, seg, sq, sk,
    docs, state, states, keys, mid, mids, own_row, rows_y, rows_x,
    gates, mixed, weights,
    load_sem, doc_send, doc_recv, state_send, state_recv, key_send, key_recv, mid_send, mid_recv,
    y_send, y_recv, x_send, x_recv,
):
    z = lax.axis_index("outer")
    c = lax.axis_index("inner")
    h = lax.axis_index("heads")
    y, x = h // x_chips, h % x_chips
    block = 2 * z + c
    blocks = 2 * groups
    tokens = q.shape[0]
    heads = q.shape[1] // DH
    head_cols = [slice(i * DH, (i + 1) * DH) for i in range(heads)]

    def place(n):
        return n // 2, n % 2

    def row_head(d):
        return y * x_chips + lax.rem(x + d, x_chips)

    def column_head(d):
        return lax.rem(y + d, y_chips) * x_chips + x

    loads = [
        pltpu.make_async_copy(a, b, load_sem.at[i])
        for i, (a, b) in enumerate(
            ((seg_in, seg), (k_in, k), (v_in, v), (q_in, q), (gain_in, gain), (g_in, g), (sk_in, sk), (sq_in, sq))
        )
    ]
    for copy in loads:
        copy.start()

    barrier = pltpu.get_barrier_semaphore()

    def greet(device):
        pl.semaphore_signal(barrier, inc=1, device_id=device, device_id_type=MESH)

    other = (z, 1 - c, h)
    has_relay = z >= 1
    pl.when(has_relay)(lambda: greet(other))
    for j in range(REACH + 1):

        @pl.when(block >= j)
        def _(j=j):
            for d in range(0 if j else 1, x_chips):
                greet((*place(block - j), row_head(d)))

    for d in range(1, y_chips):
        greet((z, c, column_head(d)))

    for j in range(1, REACH + 1):

        @pl.when(block < j)
        def _(j=j):
            docs[j - 1] = jnp.full((1, tokens), -1, jnp.int32)
            states[j - 1] = jnp.zeros(states.shape[1:], BF16)
            keys[j - 1] = jnp.zeros(keys.shape[1:], BF16)
            mids[j - 1] = jnp.zeros(mids.shape[1:], BF16)
            rows_x[j] = jnp.zeros(rows_x.shape[1:], F32)

    for copy in loads[:3]:
        copy.wait()
    doc_row = seg[...].astype(F32)
    doc_col = column(doc_row)
    kept = doc_col == doc_row[:, tokens - 1 :]
    for cols in head_cols:
        masked = jnp.where(kept, k[:, cols].astype(F32), 0.0).astype(BF16)
        state[cols, :] = matmul_tn(masked, v[:, cols]).astype(BF16)

    after = jnp.minimum(REACH, blocks - 1 - block)
    pl.semaphore_wait(
        barrier, y_chips - 1 + x_chips - 1 + after * x_chips + has_relay.astype(jnp.int32)
    )

    waits = []

    def remote(src, dst, send_sem, recv_sem, device):
        return pltpu.make_async_remote_copy(
            src_ref=src, dst_ref=dst, send_sem=send_sem, recv_sem=recv_sem, device_id=device, device_id_type=MESH
        )

    def send(condition, *args):
        copy = remote(*args)
        pl.when(condition)(copy.start)
        waits.append((condition, copy))

    def arrived(condition, dst, slot, recvs):
        pl.when(condition)(pltpu.make_async_copy(dst.at[slot], dst.at[slot], recvs.at[slot]).wait)

    relay_slot, rest_slot = 2 * c, 2 - 2 * c
    has_rest = z + 2 * c >= 2

    def spread(src, dst, sends, recvs):
        send(z + c < groups, src, dst.at[0], sends.at[0], recvs.at[0], (z + c, 1 - c, h))
        send(z + 1 + c < groups, src, dst.at[2], sends.at[1], recvs.at[2], (z + 1 + c, 1 - c, h))

    def gather(dst, sends, recvs):
        arrived(has_relay, dst, relay_slot, recvs)
        send(has_relay, dst.at[relay_slot], dst.at[1], sends.at[2], recvs.at[1], other)

    def gathered(dst, recvs):
        arrived(has_rest, dst, rest_slot, recvs)
        arrived(has_relay, dst, 1, recvs)

    for j in range(REACH):
        there = block + j + 1 < blocks
        send(there, seg, docs.at[j], doc_send.at[j], doc_recv.at[j], (*place(block + j + 1), h))
    spread(state, states, state_send, state_recv)
    loads[6].wait()
    spread(sk, keys, key_send, key_recv)

    loads[3].wait()
    at_t = lax.broadcasted_iota(jnp.int32, (tokens, tokens), 0)
    at_s = lax.broadcasted_iota(jnp.int32, (tokens, tokens), 1)
    own_seen = (at_t >= at_s) & (doc_col == doc_row)
    for cols in head_cols:
        intra = jnp.where(own_seen, matmul_nt(q[:, cols], k[:, cols]), 0.0).astype(BF16)
        mixed[:, cols] = matmul(intra, v[:, cols])
    loads[4].wait()
    loads[5].wait()
    for i, cols in enumerate(head_cols):
        gates[:, cols] = jax.nn.sigmoid(g[:, cols].astype(F32)) * gain[i : i + 1].astype(F32)

    for j in range(REACH):
        arrived(block > j, docs, j, doc_recv)

    gather(states, state_send, state_recv)
    gathered(states, state_recv)
    for cols in head_cols:
        q_f32 = q[:, cols].astype(F32)
        carried = None
        for j in range(REACH):
            last = docs[j].astype(F32)[:, tokens - 1 :]
            part = matmul(jnp.where(doc_col == last, q_f32, 0.0).astype(BF16), states[j, cols, :])
            carried = part if carried is None else carried + part
        mixed[:, cols] += carried

    square = mixed[...] * mixed[...]
    own_row[...] = matmul_nt(jnp.ones((8, heads * DH), BF16), square.astype(BF16))[:1]

    for d in range(1, y_chips):
        remote(own_row, rows_y.at[y], y_send, y_recv, (z, c, column_head(d))).start()
    rows_y[y] = own_row[...]
    mid[...] = (mixed[...] * gates[...]).astype(BF16)
    spread(mid, mids, mid_send, mid_recv)

    loads[7].wait()
    gather(keys, key_send, key_recv)
    gathered(keys, key_recv)
    scale = 1.0 / math.sqrt(DH)
    for i, cols in enumerate(head_cols):
        query = sq[:, cols]
        parts = [jnp.where(own_seen, matmul_nt(query, sk[:, cols]) * scale, -jnp.inf)]
        for j in range(REACH):
            seen = doc_col == docs[j].astype(F32)
            parts.append(jnp.where(seen, matmul_nt(query, keys[j, :, cols]) * scale, -jnp.inf))
        top = jnp.maximum(jnp.maximum(parts[0], parts[1]), jnp.maximum(parts[2], parts[3]))
        top = jnp.max(top, axis=1, keepdims=True)
        parts = [jnp.exp(part - top) for part in parts]
        total = jnp.sum(parts[0] + parts[1] + parts[2] + parts[3], axis=1, keepdims=True)
        for j, part in enumerate(parts):
            weights[i, j] = part / total

    if y_chips > 1:
        span = pl.ds(0, y_chips - 1)
        pltpu.make_async_copy(rows_y.at[span], rows_y.at[span], y_recv).wait()
    column_row = rows_x.at[0, x]
    column_row[...] = jnp.sum(rows_y[...], axis=0)
    for j in range(REACH + 1):

        @pl.when(block + j < blocks)
        def _(j=j):
            for d in range(0 if j else 1, x_chips):
                device = (*place(block + j), row_head(d))
                remote(column_row, rows_x.at[j, x], x_send.at[j], x_recv.at[j], device).start()

    gather(mids, mid_send, mid_recv)

    def x_span(j):
        return rows_x.at[j, pl.ds(0, x_chips if j else x_chips - 1)]

    def inverse_norm(j):
        pl.when(block >= j)(pltpu.make_async_copy(x_span(j), x_span(j), x_recv.at[j]).wait)
        return lax.rsqrt(jnp.sum(rows_x[j], axis=0) / total_columns + 1e-05)

    inverse = inverse_norm(0)
    inverse_col = column(inverse)
    for cols in head_cols:
        lin_out[:, cols] = (mixed[:, cols] * gates[:, cols] * inverse_col).astype(BF16)

    gathered(mids, mid_recv)
    inverses = [inverse] + [inverse_norm(j + 1) for j in range(REACH)]
    for i, cols in enumerate(head_cols):
        result = matmul((weights[i, 0] * inverses[0]).astype(BF16), mid[:, cols])
        for j in range(REACH):
            result += matmul((weights[i, j + 1] * inverses[j + 1]).astype(BF16), mids[j, :, cols])
        att_out[:, cols] = result.astype(BF16)

    for condition, copy in waits:
        pl.when(condition)(copy.wait_send)
    if y_chips > 1:
        pltpu.make_async_copy(rows_y.at[span], rows_y.at[span], y_send).wait()
    for j in range(REACH + 1):
        pl.when(block + j < blocks)(pltpu.make_async_copy(x_span(j), x_span(j), x_send.at[j]).wait)


def per_device(mesh, *args):
    q, k, v, g, gain, seg, sq, sk = args
    tokens, columns = q.shape
    groups = mesh.shape["outer"]
    x_chips = min(X_CHIPS, mesh.shape["heads"])
    y_chips = mesh.shape["heads"] // x_chips
    total_columns = columns * mesh.shape["heads"]
    seg = seg.reshape(1, tokens)
    gain = gain.reshape(columns // DH, DH)
    dma = pltpu.SemaphoreType.DMA
    block = (tokens, columns)
    stacked = (columns, DH)
    return pl.pallas_call(
        functools.partial(kernel, groups, x_chips, y_chips, total_columns),
        out_shape=(jax.ShapeDtypeStruct(block, BF16), jax.ShapeDtypeStruct(block, BF16)),
        in_specs=[pl.BlockSpec(memory_space=pl.ANY)] * 8,
        out_specs=(pl.BlockSpec(memory_space=pltpu.VMEM), pl.BlockSpec(memory_space=pltpu.VMEM)),
        scratch_shapes=[
            pltpu.VMEM(block, BF16), pltpu.VMEM(block, BF16), pltpu.VMEM(block, BF16), pltpu.VMEM(block, BF16),
            pltpu.VMEM((columns // DH, DH), BF16), pltpu.VMEM((1, tokens), jnp.int32),
            pltpu.VMEM(block, BF16), pltpu.VMEM(block, BF16),
            pltpu.VMEM((REACH, 1, tokens), jnp.int32),
            pltpu.VMEM(stacked, BF16), pltpu.VMEM((REACH,) + stacked, BF16),
            pltpu.VMEM((REACH,) + block, BF16),
            pltpu.VMEM(block, BF16), pltpu.VMEM((REACH,) + block, BF16),
            pltpu.VMEM((1, tokens), F32),
            pltpu.VMEM((y_chips, 1, tokens), F32),
            pltpu.VMEM((REACH + 1, x_chips, 1, tokens), F32),
            pltpu.VMEM(block, F32), pltpu.VMEM(block, F32),
            pltpu.VMEM((columns // DH, REACH + 1, tokens, tokens), F32),
            dma((8,)),
            dma((REACH,)), dma((REACH,)), dma((3,)), dma((REACH,)), dma((3,)), dma((REACH,)), dma((3,)), dma((REACH,)),
            dma, dma, dma((REACH + 1,)), dma((REACH + 1,)),
        ],
        compiler_params=pltpu.CompilerParams(collective_id=0, has_side_effects=True),
    )(q, k, v, g, gain, seg, sq, sk)


def solution(mesh):
    block = P(("outer", "inner"), "heads")
    return jax.shard_map(
        functools.partial(per_device, mesh),
        mesh=mesh,
        in_specs=(block, block, block, block, P("heads"), P(("outer", "inner")), block, block),
        out_specs=(block, block),
        check_vma=False,
    )
```

time: 39.6 us -> 26.7 us (0.67)
  the two profiles are of different devices: /device:TPU:1 before, /device:TPU:576 now
where the time goes in v2:
time: 26.7 us; the launch traced here: 26.4 us
  Pallas kernels  23.6 us (88%)
  local copies, waits for them, and re-layouts  2.14 us (8%)
  between operations  0.65 us (2%)
    pallas_call x1, Pallas kernels, per_device(): pl.pallas_call(functools.partial(kernel, groups, x_chips, y_chips, total_...  23.6 us
    unnamed x4, local copies, waits for them, and re-layouts  2.14 us

profile of v2, /device:TPU:576, one launch (start us, length us, event | category | flops | bytes accessed | tf_op | source)
XLA Modules:
  0.0 26.4 jit_solution(5574319630706501966)
XLA Ops:
  0.6 23.6 %shard_map.95 = (bf16[128,256]{1,0:T(8,128)(2,1)}, bf16[128,256]{1,0:T(8,128)(2,1)}) custom-call(bf16[128,256]{1,0:T(8,128)(2,1)} %q_in.1, bf16[128,256]{1,0:T(8,128)(2,1)} %k_in.1, bf16[128,256]{1,0:T(8,128)(2,1)} %v_in.1, bf16[128,256]{1,0:T(8,128)(2,1)} %g_in.1, bf16[2,128]{1,0:T(2,128)(2,1)} %bitcast.2, s32[1,128]{1,0:T(1,128)} %bitcast.3, ...), custom_call_target="tpu_custom_call" | custom-call | tf_op jit(solution)/shard_map/pallas_call | solution.py:260
  24.2 0.0 copy-start
  24.2 1.5 %copy.12 = bf16[128,256]{1,0:T(8,128)(2,1)} copy(bf16[128,256]{1,0:T(8,128)(2,1)} %get-tuple-element.4) | data formatting | bytes 131072
  25.7 0.0 copy-done
  25.7 0.6 %copy.13 = bf16[128,256]{1,0:T(8,128)(2,1)} copy(bf16[128,256]{1,0:T(8,128)(2,1)S(1)} %copy-done) | data formatting | bytes 131072
Async XLA Ops:
  24.2 1.5 %copy-start = (bf16[128,256]{1,0:T(8,128)(2,1)S(1)}, bf16[128,256]{1,0:T(8,128)(2,1)}, u32[]{:S(2)}) copy-start(bf16[128,256]{1,0:T(8,128)(2,1)} %get-tuple-element.5) | copy-start | bytes 196612

commit v3 on v2

v3 whole, which is shorter than its diff:
```python
import functools
import math

import jax
import jax.numpy as jnp
from jax import lax
from jax.experimental import pallas as pl
from jax.experimental.pallas import tpu as pltpu
from jax.sharding import PartitionSpec as P

DH = 128
X_CHIPS = 4
REACH = 3
MESH = pl.DeviceIdType.MESH
F32 = jnp.float32
BF16 = jnp.bfloat16


def matmul(a, b):
    return jnp.dot(a, b, preferred_element_type=F32)


def matmul_nt(a, b):
    return lax.dot_general(a, b, (((1,), (1,)), ((), ())), preferred_element_type=F32)


def matmul_tn(a, b):
    return lax.dot_general(a, b, (((0,), (0,)), ((), ())), preferred_element_type=F32)


def column(row):
    n = row.shape[1]
    return jnp.transpose(jnp.broadcast_to(row, (n, n)))


def kernel(
    groups, x_chips, y_chips, total_columns,
    q_in, k_in, v_in, g_in, gain_in, seg_in, sq_in, sk_in,
    out,
    q, k, v, g, gain, seg, sq, sk,
    state, states, keys, mid, mids, own_row, rows_y, rows_x,
    gates, mixed, weights,
    load_sem, state_send, state_recv, key_send, key_recv, mid_send, mid_recv,
    y_send, y_recv, x_send, x_recv, hop_sem, ring_sem, later_sem,
):
    z = lax.axis_index("outer")
    c = lax.axis_index("inner")
    h = lax.axis_index("heads")
    y, x = h // x_chips, h % x_chips
    block = 2 * z + c
    blocks = 2 * groups
    tokens = q.shape[0]
    heads = q.shape[1] // DH
    head_cols = [slice(i * DH, (i + 1) * DH) for i in range(heads)]

    def place(n):
        return n // 2, n % 2

    def row_head(d):
        return y * x_chips + lax.rem(x + d, x_chips)

    def column_head(d):
        return lax.rem(y + d, y_chips) * x_chips + x

    other = (z, 1 - c, h)
    has_relay = z >= 1
    barrier = pltpu.get_barrier_semaphore()

    def signal(sem, device):
        pl.semaphore_signal(sem, inc=1, device_id=device, device_id_type=MESH)

    def signal_if(condition, sem, device):
        pl.when(condition)(lambda: signal(sem, device))

    loads = [
        pltpu.make_async_copy(a, b, load_sem.at[i])
        for i, (a, b) in enumerate(
            ((seg_in, seg), (k_in, k), (v_in, v), (q_in, q), (gain_in, gain), (g_in, g), (sk_in, sk), (sq_in, sq))
        )
    ]
    for copy in loads[:3]:
        copy.start()

    near_blocks = [
        (block >= 1, block - 1), (block >= 2, block - 2), (block + 1 < blocks, block + 1), (block + 2 < blocks, block + 2),
        ((c == 1) & (block >= 3), block - 3), ((c == 0) & (block + 3 < blocks), block + 3),
    ]
    near_heads = [row_head(d) for d in range(1, x_chips)] + [column_head(d) for d in (1, y_chips - 1, 2, y_chips - 2)]
    for condition, n in near_blocks:
        signal_if(condition, barrier, (*place(n), h))
    for head in near_heads:
        signal(barrier, (z, c, head))
    for copy in loads[3:]:
        copy.start()

    columns = heads * DH
    for j in range(1, REACH + 1):

        @pl.when(block < j)
        def _(j=j):
            states[j - 1, :columns] = jnp.zeros((columns, DH), BF16)
            states[j - 1, columns:] = jnp.full((states.shape[1] - columns, DH), -1.0, BF16)
            keys[j - 1] = jnp.zeros(keys.shape[1:], BF16)
            mids[j - 1] = jnp.zeros(mids.shape[1:], BF16)
            rows_x[j] = jnp.zeros(rows_x.shape[1:], F32)

    for copy in loads[:3]:
        copy.wait()
    doc_row = seg[...].astype(F32)
    doc_col = column(doc_row)
    kept = doc_col == doc_row[:, tokens - 1 :]
    for cols in head_cols:
        masked = jnp.where(kept, k[:, cols].astype(F32), 0.0).astype(BF16)
        state[cols, :] = matmul_tn(masked, v[:, cols]).astype(BF16)

    state[columns:, :] = jnp.broadcast_to(doc_row, (state.shape[0] - columns, tokens)).astype(BF16)

    def count(*conditions):
        return sum(condition.astype(jnp.int32) for condition in conditions)

    pl.semaphore_wait(barrier, len(near_heads) + count(*[condition for condition, _ in near_blocks]))

    middle = (c == 0) & (z >= 1) & (z + 1 < groups)
    signal_if(middle, hop_sem, (z - 1, 1, h))
    signal_if(middle, hop_sem, (z + 1, 0, h))

    waits = []

    def remote(src, dst, send_sem, recv_sem, device):
        return pltpu.make_async_remote_copy(
            src_ref=src, dst_ref=dst, send_sem=send_sem, recv_sem=recv_sem, device_id=device, device_id_type=MESH
        )

    def send(condition, *args):
        copy = remote(*args)
        pl.when(condition)(copy.start)
        waits.append((condition, copy))

    def arrived(condition, dst, slot, recvs):
        pl.when(condition)(pltpu.make_async_copy(dst.at[slot], dst.at[slot], recvs.at[slot]).wait)

    relay_slot, rest_slot = 2 * c, 2 - 2 * c
    has_rest = z + 2 * c >= 2

    def send_near(src, dst, sends, recvs):
        send(z + c < groups, src, dst.at[0], sends.at[0], recvs.at[0], (z + c, 1 - c, h))

    def send_far(src, dst, sends, recvs, condition=True):
        there = condition & (z + 1 + c < groups)
        send(there, src, dst.at[2], sends.at[1], recvs.at[2], (z + 1 + c, 1 - c, h))

    def spread(src, dst, sends, recvs):
        send_near(src, dst, sends, recvs)
        send_far(src, dst, sends, recvs)

    def gather(dst, sends, recvs):
        arrived(has_relay, dst, relay_slot, recvs)
        send(has_relay, dst.at[relay_slot], dst.at[1], sends.at[2], recvs.at[1], other)

    def gathered(dst, recvs):
        arrived(has_rest, dst, rest_slot, recvs)
        arrived(has_relay, dst, 1, recvs)

    send_near(state, states, state_send, state_recv)
    send_far(state, states, state_send, state_recv, c == 0)
    for d in (2, y_chips - 2):
        signal(ring_sem, (z, c, column_head(d)))
    for j in range(1, REACH + 1):
        signal_if((block >= j) & ((c == 1) if j == REACH else True), later_sem, (*place(block - j), h))

    loads[3].wait()
    at_t = lax.broadcasted_iota(jnp.int32, (tokens, tokens), 0)
    at_s = lax.broadcasted_iota(jnp.int32, (tokens, tokens), 1)
    own_seen = (at_t >= at_s) & (doc_col == doc_row)
    for cols in head_cols:
        intra = jnp.where(own_seen, matmul_nt(q[:, cols], k[:, cols]), 0.0).astype(BF16)
        mixed[:, cols] = matmul(intra, v[:, cols])
    loads[4].wait()
    loads[5].wait()
    for i, cols in enumerate(head_cols):
        gates[:, cols] = jax.nn.sigmoid(g[:, cols].astype(F32)) * gain[i : i + 1].astype(F32)

    pl.when(((c == 0) & (z >= 2)) | ((c == 1) & (z + 2 < groups)))(lambda: pl.semaphore_wait(hop_sem, 1))
    send_far(state, states, state_send, state_recv, c == 1)
    signal_if((c == 0) & (z >= 2), later_sem, (z - 2, 1, h))
    loads[6].wait()
    spread(sk, keys, key_send, key_recv)

    gather(states, state_send, state_recv)
    gathered(states, state_recv)
    doc_rows = [states[j, columns : columns + 1, :].astype(F32) for j in range(REACH)]
    for cols in head_cols:
        q_f32 = q[:, cols].astype(F32)
        carried = None
        for j in range(REACH):
            last = doc_rows[j][:, tokens - 1 :]
            part = matmul(jnp.where(doc_col == last, q_f32, 0.0).astype(BF16), states[j, cols, :])
            carried = part if carried is None else carried + part
        mixed[:, cols] += carried

    square = mixed[...] * mixed[...]
    own_row[...] = matmul_nt(jnp.ones((8, heads * DH), BF16), square.astype(BF16))[:1]

    pl.semaphore_wait(ring_sem, 2)
    for d in range(1, y_chips):
        remote(own_row, rows_y.at[y], y_send, y_recv, (z, c, column_head(d))).start()
    rows_y[y] = own_row[...]
    mid[...] = (mixed[...] * gates[...]).astype(BF16)
    spread(mid, mids, mid_send, mid_recv)
    gather(keys, key_send, key_recv)

    y_span = rows_y.at[pl.ds(0, y_chips - 1)]
    pltpu.make_async_copy(y_span, y_span, y_recv).wait()
    column_row = rows_x.at[0, x]
    column_row[...] = jnp.sum(rows_y[...], axis=0)
    after = jnp.minimum(REACH, blocks - 1 - block)
    pl.when(after > 0)(lambda: pl.semaphore_wait(later_sem, after))
    for j in range(REACH + 1):

        @pl.when(block + j < blocks)
        def _(j=j):
            for d in range(0 if j else 1, x_chips):
                device = (*place(block + j), row_head(d))
                remote(column_row, rows_x.at[j, x], x_send.at[j], x_recv.at[j], device).start()

    gather(mids, mid_send, mid_recv)

    loads[7].wait()
    gathered(keys, key_recv)
    scale = 1.0 / math.sqrt(DH)
    for i, cols in enumerate(head_cols):
        query = sq[:, cols]
        parts = [jnp.where(own_seen, matmul_nt(query, sk[:, cols]) * scale, -jnp.inf)]
        for j in range(REACH):
            seen = doc_col == doc_rows[j]
            parts.append(jnp.where(seen, matmul_nt(query, keys[j, :, cols]) * scale, -jnp.inf))
        top = jnp.maximum(jnp.maximum(parts[0], parts[1]), jnp.maximum(parts[2], parts[3]))
        top = jnp.max(top, axis=1, keepdims=True)
        parts = [jnp.exp(part - top) for part in parts]
        total = jnp.sum(parts[0] + parts[1] + parts[2] + parts[3], axis=1, keepdims=True)
        for j, part in enumerate(parts):
            weights[i, j] = part / total

    def x_span(j):
        return rows_x.at[j, pl.ds(0, x_chips if j else x_chips - 1)]

    def inverse_norm(j):
        pl.when(block >= j)(pltpu.make_async_copy(x_span(j), x_span(j), x_recv.at[j]).wait)
        return lax.rsqrt(jnp.sum(rows_x[j], axis=0) / total_columns + 1e-05)

    inverse = inverse_norm(0)
    inverse_col = column(inverse)
    for cols in head_cols:
        out[0, :, cols] = (mixed[:, cols] * gates[:, cols] * inverse_col).astype(BF16)

    gathered(mids, mid_recv)
    inverses = [inverse] + [inverse_norm(j + 1) for j in range(REACH)]
    for i, cols in enumerate(head_cols):
        result = matmul((weights[i, 0] * inverses[0]).astype(BF16), mid[:, cols])
        for j in range(REACH):
            result += matmul((weights[i, j + 1] * inverses[j + 1]).astype(BF16), mids[j, :, cols])
        out[1, :, cols] = result.astype(BF16)

    for condition, copy in waits:
        pl.when(condition)(copy.wait_send)
    pltpu.make_async_copy(y_span, y_span, y_send).wait()
    for j in range(REACH + 1):
        pl.when(block + j < blocks)(pltpu.make_async_copy(x_span(j), x_span(j), x_send.at[j]).wait)


def per_device(mesh, *args):
    q, k, v, g, gain, seg, sq, sk = args
    tokens, columns = q.shape
    groups = mesh.shape["outer"]
    x_chips = min(X_CHIPS, mesh.shape["heads"])
    y_chips = mesh.shape["heads"] // x_chips
    total_columns = columns * mesh.shape["heads"]
    seg = seg.reshape(1, tokens)
    gain = gain.reshape(columns // DH, DH)
    dma = pltpu.SemaphoreType.DMA
    regular = pltpu.SemaphoreType.REGULAR
    block = (tokens, columns)
    stacked = (columns + 16, DH)
    outs = pl.pallas_call(
        functools.partial(kernel, groups, x_chips, y_chips, total_columns),
        out_shape=pltpu.VMEM((2,) + block, BF16),
        in_specs=[pl.BlockSpec(memory_space=pl.ANY)] * 8,
        out_specs=pl.BlockSpec(memory_space=pltpu.VMEM),
        scratch_shapes=[
            pltpu.VMEM(block, BF16), pltpu.VMEM(block, BF16), pltpu.VMEM(block, BF16), pltpu.VMEM(block, BF16),
            pltpu.VMEM((columns // DH, DH), BF16), pltpu.VMEM((1, tokens), jnp.int32),
            pltpu.VMEM(block, BF16), pltpu.VMEM(block, BF16),
            pltpu.VMEM(stacked, BF16), pltpu.VMEM((REACH,) + stacked, BF16),
            pltpu.VMEM((REACH,) + block, BF16),
            pltpu.VMEM(block, BF16), pltpu.VMEM((REACH,) + block, BF16),
            pltpu.VMEM((1, tokens), F32),
            pltpu.VMEM((y_chips, 1, tokens), F32),
            pltpu.VMEM((REACH + 1, x_chips, 1, tokens), F32),
            pltpu.VMEM(block, F32), pltpu.VMEM(block, F32),
            pltpu.VMEM((columns // DH, REACH + 1, tokens, tokens), F32),
            dma((8,)),
            dma((3,)), dma((REACH,)), dma((3,)), dma((REACH,)), dma((3,)), dma((REACH,)),
            dma, dma, dma((REACH + 1,)), dma((REACH + 1,)),
            regular, regular, regular,
        ],
        compiler_params=pltpu.CompilerParams(collective_id=0, has_side_effects=True),
    )(q, k, v, g, gain, seg, sq, sk)
    return outs[0], outs[1]


def solution(mesh):
    block = P(("outer", "inner"), "heads")
    return jax.shard_map(
        functools.partial(per_device, mesh),
        mesh=mesh,
        in_specs=(block, block, block, block, P("heads"), P(("outer", "inner")), block, block),
        out_specs=(block, block),
        check_vma=False,
    )
```

time: 26.7 us -> 23.5 us (0.88)
  the two profiles are of different devices: /device:TPU:576 before, /device:TPU:1 now
where the time goes in v3:
time: 23.5 us; the launch traced here: 23.3 us
  Pallas kernels  22 us (94%)
  local copies, waits for them, and re-layouts  0.66 us (3%)
  between operations  0.64 us (3%)
    pallas_call x1, Pallas kernels, per_device(): pl.pallas_call(functools.partial(kernel, groups, x_chips, y_chips, total_...  22 us
    squeeze x1, local copies, waits for them, and re-layouts, per_device(): return (outs[0], outs[1])  0.66 us

profile of v3, /device:TPU:1, one launch (start us, length us, event | category | flops | bytes accessed | tf_op | source)
XLA Modules:
  0.0 23.3 jit_solution(8653837511791957988)
XLA Ops:
  0.6 22.0 %shard_map.95 = bf16[2,128,256]{2,1,0:T(8,128)(2,1)S(1)} custom-call(bf16[128,256]{1,0:T(8,128)(2,1)} %q_in.1, bf16[128,256]{1,0:T(8,128)(2,1)} %k_in.1, bf16[128,256]{1,0:T(8,128)(2,1)} %v_in.1, bf16[128,256]{1,0:T(8,128)(2,1)} %g_in.1, bf16[2,128]{1,0:T(2,128)(2,1)} %bitcast.6, s32[1,128]{1,0:T(1,128)} %bitcast.7, bf16[128,256]{1,0:T(8,128)(2,1)} %sq_in.1, ...), custom_call_target="tpu_custom_call" | custom-call | tf_op jit(solution)/shard_map/pallas_call | solution.py:284
  22.7 0.7 %slice_bitcast_fusion = (bf16[128,256]{1,0:T(8,128)(2,1)}, bf16[128,256]{1,0:T(8,128)(2,1)}) fusion(bf16[2,128,256]{2,1,0:T(8,128)(2,1)S(1)} %shard_map.95), kind=kLoop, calls=%fused_computation | loop fusion | bytes 262144 | tf_op jit(solution)/shard_map/squeeze | solution.py:308

commit v4 on v3

--- a/solution.py
+++ b/solution.py
@@ -41,7 +41,7 @@
     state, states, keys, mid, mids, own_row, rows_y, rows_x,
     gates, mixed, weights,
     load_sem, state_send, state_recv, key_send, key_recv, mid_send, mid_recv,
-    y_send, y_recv, x_send, x_recv, hop_sem, ring_sem, later_sem,
+    y_send, y_recv, x_send, x_recv, hop_sem, ring_sem, later_sem, go_sem,
 ):
     z = lax.axis_index("outer")
     c = lax.axis_index("inner")
@@ -81,15 +81,19 @@
     for copy in loads[:3]:
         copy.start()
 
-    near_blocks = [
-        (block >= 1, block - 1), (block >= 2, block - 2), (block + 1 < blocks, block + 1), (block + 2 < blocks, block + 2),
-        ((c == 1) & (block >= 3), block - 3), ((c == 0) & (block + 3 < blocks), block + 3),
-    ]
+    first = block == 0
+    earlier = [(True, block - 1), (True, block - 2), (c == 1, block - 3)]
+    later = [(True, block + 1), (True, block + 2), (c == 0, block + 3)]
+    reached = [(near & (n >= 1), n) for near, n in earlier] + [(near & (n < blocks), n) for near, n in later]
+    heard = [near & (n >= 0) for near, n in earlier] + [near & (n < blocks) & (block > 0) for near, n in later]
     near_heads = [row_head(d) for d in range(1, x_chips)] + [column_head(d) for d in (1, y_chips - 1, 2, y_chips - 2)]
-    for condition, n in near_blocks:
+    for condition, n in reached:
         signal_if(condition, barrier, (*place(n), h))
     for head in near_heads:
         signal(barrier, (z, c, head))
+    far_heads = [column_head(d) for d in range(3, y_chips - 2)]
+    for head in far_heads:
+        signal_if(first, barrier, (z, c, head))
     for copy in loads[3:]:
         copy.start()
 
@@ -118,7 +122,9 @@
     def count(*conditions):
         return sum(condition.astype(jnp.int32) for condition in conditions)
 
-    pl.semaphore_wait(barrier, len(near_heads) + count(*[condition for condition, _ in near_blocks]))
+    pl.when(block > 0)(lambda: pl.semaphore_wait(barrier, len(near_heads) + count(*heard)))
+    pl.when(first)(lambda: pl.semaphore_wait(go_sem, 1))
+    signal_if(block == 1, go_sem, other)
 
     middle = (c == 0) & (z >= 1) & (z + 1 < groups)
     signal_if(middle, hop_sem, (z - 1, 1, h))
@@ -164,7 +170,7 @@
     send_near(state, states, state_send, state_recv)
     send_far(state, states, state_send, state_recv, c == 0)
     for d in (2, y_chips - 2):
-        signal(ring_sem, (z, c, column_head(d)))
+        signal_if(block > 0, ring_sem, (z, c, column_head(d)))
     for j in range(1, REACH + 1):
         signal_if((block >= j) & ((c == 1) if j == REACH else True), later_sem, (*place(block - j), h))
 
@@ -183,11 +189,10 @@
     pl.when(((c == 0) & (z >= 2)) | ((c == 1) & (z + 2 < groups)))(lambda: pl.semaphore_wait(hop_sem, 1))
     send_far(state, states, state_send, state_recv, c == 1)
     signal_if((c == 0) & (z >= 2), later_sem, (z - 2, 1, h))
+    gather(states, state_send, state_recv)
+    gathered(states, state_recv)
     loads[6].wait()
     spread(sk, keys, key_send, key_recv)
-
-    gather(states, state_send, state_recv)
-    gathered(states, state_recv)
     doc_rows = [states[j, columns : columns + 1, :].astype(F32) for j in range(REACH)]
     for cols in head_cols:
         q_f32 = q[:, cols].astype(F32)
@@ -201,7 +206,8 @@
     square = mixed[...] * mixed[...]
     own_row[...] = matmul_nt(jnp.ones((8, heads * DH), BF16), square.astype(BF16))[:1]
 
-    pl.semaphore_wait(ring_sem, 2)
+    pl.when(block > 0)(lambda: pl.semaphore_wait(ring_sem, 2))
+    pl.when(first)(lambda: pl.semaphore_wait(barrier, len(near_heads) + len(far_heads)))
     for d in range(1, y_chips):
         remote(own_row, rows_y.at[y], y_send, y_recv, (z, c, column_head(d))).start()
     rows_y[y] = own_row[...]
@@ -253,12 +259,15 @@
     for cols in head_cols:
         out[0, :, cols] = (mixed[:, cols] * gates[:, cols] * inverse_col).astype(BF16)
 
+    def attend(j, values):
+        norm = inverse if j == 0 else inverse_norm(j)
+        return [matmul((weights[i, j] * norm).astype(BF16), values[:, cols]) for i, cols in enumerate(head_cols)]
+
+    results = attend(0, mid)
     gathered(mids, mid_recv)
-    inverses = [inverse] + [inverse_norm(j + 1) for j in range(REACH)]
-    for i, cols in enumerate(head_cols):
-        result = matmul((weights[i, 0] * inverses[0]).astype(BF16), mid[:, cols])
-        for j in range(REACH):
-            result += matmul((weights[i, j + 1] * inverses[j + 1]).astype(BF16), mids[j, :, cols])
+    for j in range(REACH, 0, -1):
+        results = [result + part for result, part in zip(results, attend(j, mids.at[j - 1]))]
+    for result, cols in zip(results, head_cols):
         out[1, :, cols] = result.astype(BF16)
 
     for condition, copy in waits:
@@ -301,7 +310,7 @@
             dma((8,)),
             dma((3,)), dma((REACH,)), dma((3,)), dma((REACH,)), dma((3,)), dma((REACH,)),
             dma, dma, dma((REACH + 1,)), dma((REACH + 1,)),
-            regular, regular, regular,
+            regular, regular, regular, regular,
         ],
         compiler_params=pltpu.CompilerParams(collective_id=0, has_side_effects=True),
     )(q, k, v, g, gain, seg, sq, sk)

time: 23.5 us -> 22.8 us (0.970)
  the two profiles are of different devices: /device:TPU:1 before, /device:TPU:576 now
where the time goes in v4:
time: 22.8 us; the launch traced here: 22.7 us
  Pallas kernels  21.4 us (94%)
  local copies, waits for them, and re-layouts  0.66 us (3%)
  between operations  0.64 us (3%)
    pallas_call x1, Pallas kernels, per_device(): pl.pallas_call(functools.partial(kernel, groups, x_chips, y_chips, total_...  21.4 us
    squeeze x1, local copies, waits for them, and re-layouts, per_device(): return (outs[0], outs[1])  0.66 us

profile of v4, /device:TPU:576, one launch (start us, length us, event | category | flops | bytes accessed | tf_op | source)
XLA Modules:
  0.0 22.7 jit_solution(5674506079228612436)
XLA Ops:
  0.6 21.4 %shard_map.95 = bf16[2,128,256]{2,1,0:T(8,128)(2,1)S(1)} custom-call(bf16[128,256]{1,0:T(8,128)(2,1)} %q_in.1, bf16[128,256]{1,0:T(8,128)(2,1)} %k_in.1, bf16[128,256]{1,0:T(8,128)(2,1)} %v_in.1, bf16[128,256]{1,0:T(8,128)(2,1)} %g_in.1, bf16[2,128]{1,0:T(2,128)(2,1)} %bitcast.6, s32[1,128]{1,0:T(1,128)} %bitcast.7, bf16[128,256]{1,0:T(8,128)(2,1)} %sq_in.1, ...), custom_call_target="tpu_custom_call" | custom-call | tf_op jit(solution)/shard_map/pallas_call | solution.py:293
  22.0 0.7 %slice_bitcast_fusion = (bf16[128,256]{1,0:T(8,128)(2,1)}, bf16[128,256]{1,0:T(8,128)(2,1)}) fusion(bf16[2,128,256]{2,1,0:T(8,128)(2,1)S(1)} %shard_map.95), kind=kLoop, calls=%fused_computation | loop fusion | bytes 262144 | tf_op jit(solution)/shard_map/squeeze | solution.py:317

commit v5 on v4

--- a/solution.py
+++ b/solution.py
@@ -159,9 +159,10 @@
         send_near(src, dst, sends, recvs)
         send_far(src, dst, sends, recvs)
 
-    def gather(dst, sends, recvs):
-        arrived(has_relay, dst, relay_slot, recvs)
-        send(has_relay, dst.at[relay_slot], dst.at[1], sends.at[2], recvs.at[1], other)
+    def gather(dst, sends, recvs, condition=True):
+        here = has_relay & condition
+        arrived(here, dst, relay_slot, recvs)
+        send(here, dst.at[relay_slot], dst.at[1], sends.at[2], recvs.at[1], other)
 
     def gathered(dst, recvs):
         arrived(has_rest, dst, rest_slot, recvs)
@@ -213,7 +214,7 @@
     rows_y[y] = own_row[...]
     mid[...] = (mixed[...] * gates[...]).astype(BF16)
     spread(mid, mids, mid_send, mid_recv)
-    gather(keys, key_send, key_recv)
+    gather(keys, key_send, key_recv, c == 0)
 
     y_span = rows_y.at[pl.ds(0, y_chips - 1)]
     pltpu.make_async_copy(y_span, y_span, y_recv).wait()
@@ -229,6 +230,7 @@
                 device = (*place(block + j), row_head(d))
                 remote(column_row, rows_x.at[j, x], x_send.at[j], x_recv.at[j], device).start()
 
+    gather(keys, key_send, key_recv, c == 1)
     gather(mids, mid_send, mid_recv)
 
     loads[7].wait()

time: 22.8 us -> 22.8 us (level)
  no operation moved by 1% of the time
where the time goes in v5:
time: 22.8 us; the launch traced here: 22.7 us
  Pallas kernels  21.4 us (94%)
  local copies, waits for them, and re-layouts  0.66 us (3%)
  between operations  0.64 us (3%)
    pallas_call x1, Pallas kernels, per_device(): pl.pallas_call(functools.partial(kernel, groups, x_chips, y_chips, total_...  21.4 us
    squeeze x1, local copies, waits for them, and re-layouts, per_device(): return (outs[0], outs[1])  0.66 us

profile of v5, /device:TPU:576, one launch (start us, length us, event | category | flops | bytes accessed | tf_op | source)
XLA Modules:
  0.0 22.7 jit_solution(6107499075152960939)
XLA Ops:
  0.6 21.4 %shard_map.95 = bf16[2,128,256]{2,1,0:T(8,128)(2,1)S(1)} custom-call(bf16[128,256]{1,0:T(8,128)(2,1)} %q_in.1, bf16[128,256]{1,0:T(8,128)(2,1)} %k_in.1, bf16[128,256]{1,0:T(8,128)(2,1)} %v_in.1, bf16[128,256]{1,0:T(8,128)(2,1)} %g_in.1, bf16[2,128]{1,0:T(2,128)(2,1)} %bitcast.6, s32[1,128]{1,0:T(1,128)} %bitcast.7, bf16[128,256]{1,0:T(8,128)(2,1)} %sq_in.1, ...), custom_call_target="tpu_custom_call" | custom-call | tf_op jit(solution)/shard_map/pallas_call | solution.py:295
  22.0 0.7 %slice_bitcast_fusion = (bf16[128,256]{1,0:T(8,128)(2,1)}, bf16[128,256]{1,0:T(8,128)(2,1)}) fusion(bf16[2,128,256]{2,1,0:T(8,128)(2,1)S(1)} %shard_map.95), kind=kLoop, calls=%fused_computation | loop fusion | bytes 262144 | tf_op jit(solution)/shard_map/squeeze | solution.py:319

commit v6 on v5

--- a/solution.py
+++ b/solution.py
@@ -196,11 +196,10 @@
     spread(sk, keys, key_send, key_recv)
     doc_rows = [states[j, columns : columns + 1, :].astype(F32) for j in range(REACH)]
     for cols in head_cols:
-        q_f32 = q[:, cols].astype(F32)
         carried = None
         for j in range(REACH):
             last = doc_rows[j][:, tokens - 1 :]
-            part = matmul(jnp.where(doc_col == last, q_f32, 0.0).astype(BF16), states[j, cols, :])
+            part = jnp.where(doc_col == last, matmul(q[:, cols], states[j, cols, :]), 0.0)
             carried = part if carried is None else carried + part
         mixed[:, cols] += carried
 
@@ -209,7 +208,7 @@
 
     pl.when(block > 0)(lambda: pl.semaphore_wait(ring_sem, 2))
     pl.when(first)(lambda: pl.semaphore_wait(barrier, len(near_heads) + len(far_heads)))
-    for d in range(1, y_chips):
+    for d in sorted(range(1, y_chips), key=lambda d: abs(d - y_chips // 2)):
         remote(own_row, rows_y.at[y], y_send, y_recv, (z, c, column_head(d))).start()
     rows_y[y] = own_row[...]
     mid[...] = (mixed[...] * gates[...]).astype(BF16)
@@ -226,7 +225,7 @@
 
         @pl.when(block + j < blocks)
         def _(j=j):
-            for d in range(0 if j else 1, x_chips):
+            for d in (2, 1, 3) + ((0,) if j else ()):
                 device = (*place(block + j), row_head(d))
                 remote(column_row, rows_x.at[j, x], x_send.at[j], x_recv.at[j], device).start()
 
@@ -252,23 +251,23 @@
     def x_span(j):
         return rows_x.at[j, pl.ds(0, x_chips if j else x_chips - 1)]
 
-    def inverse_norm(j):
+    def attend(j, norm, values):
+        return [matmul((weights[i, j] * norm).astype(BF16), values[:, cols]) for i, cols in enumerate(head_cols)]
+
+    def both(left, right):
+        return [one + other_one for one, other_one in zip(left, right)]
+
+    gathered(mids, mid_recv)
+    for j in range(REACH + 1):
         pl.when(block >= j)(pltpu.make_async_copy(x_span(j), x_span(j), x_recv.at[j]).wait)
-        return lax.rsqrt(jnp.sum(rows_x[j], axis=0) / total_columns + 1e-05)
-
-    inverse = inverse_norm(0)
+    norms = [lax.rsqrt(jnp.sum(rows_x[j], axis=0) / total_columns + 1e-05) for j in range(REACH + 1)]
+    inverse = norms[0]
+    results = attend(0, inverse, mid)
+    for j in range(1, REACH + 1):
+        results = both(results, attend(j, norms[j], mids.at[j - 1]))
     inverse_col = column(inverse)
     for cols in head_cols:
         out[0, :, cols] = (mixed[:, cols] * gates[:, cols] * inverse_col).astype(BF16)
-
-    def attend(j, values):
-        norm = inverse if j == 0 else inverse_norm(j)
-        return [matmul((weights[i, j] * norm).astype(BF16), values[:, cols]) for i, cols in enumerate(head_cols)]
-
-    results = attend(0, mid)
-    gathered(mids, mid_recv)
-    for j in range(REACH, 0, -1):
-        results = [result + part for result, part in zip(results, attend(j, mids.at[j - 1]))]
     for result, cols in zip(results, head_cols):
         out[1, :, cols] = result.astype(BF16)
 

time: 22.8 us -> 22.6 us (level)
  the two profiles are of different devices: /device:TPU:576 before, /device:TPU:641 now
where the time goes in v6:
time: 22.6 us; the launch traced here: 22.4 us
  Pallas kernels  21.1 us (93%)
  local copies, waits for them, and re-layouts  0.66 us (3%)
  between operations  0.64 us (3%)
    pallas_call x1, Pallas kernels, per_device(): pl.pallas_call(functools.partial(kernel, groups, x_chips, y_chips, total_...  21.1 us
    squeeze x1, local copies, waits for them, and re-layouts, per_device(): return (outs[0], outs[1])  0.66 us

profile of v6, /device:TPU:641, one launch (start us, length us, event | category | flops | bytes accessed | tf_op | source)
XLA Modules:
  0.0 22.4 jit_solution(3511051228889279527)
XLA Ops:
  0.6 21.1 %shard_map.95 = bf16[2,128,256]{2,1,0:T(8,128)(2,1)S(1)} custom-call(bf16[128,256]{1,0:T(8,128)(2,1)} %q_in.1, bf16[128,256]{1,0:T(8,128)(2,1)} %k_in.1, bf16[128,256]{1,0:T(8,128)(2,1)} %v_in.1, bf16[128,256]{1,0:T(8,128)(2,1)} %g_in.1, bf16[2,128]{1,0:T(2,128)(2,1)} %bitcast.6, s32[1,128]{1,0:T(1,128)} %bitcast.7, bf16[128,256]{1,0:T(8,128)(2,1)} %sq_in.1, ...), custom_call_target="tpu_custom_call" | custom-call | tf_op jit(solution)/shard_map/pallas_call | solution.py:294
  21.8 0.7 %slice_bitcast_fusion = (bf16[128,256]{1,0:T(8,128)(2,1)}, bf16[128,256]{1,0:T(8,128)(2,1)}) fusion(bf16[2,128,256]{2,1,0:T(8,128)(2,1)S(1)} %shard_map.95), kind=kLoop, calls=%fused_computation | loop fusion | bytes 262144 | tf_op jit(solution)/shard_map/squeeze | solution.py:318

commit v7 on v6

--- a/solution.py
+++ b/solution.py
@@ -41,7 +41,7 @@
     state, states, keys, mid, mids, own_row, rows_y, rows_x,
     gates, mixed, weights,
     load_sem, state_send, state_recv, key_send, key_recv, mid_send, mid_recv,
-    y_send, y_recv, x_send, x_recv, hop_sem, ring_sem, later_sem, go_sem,
+    y_send, y_recv, x_send, x_recv, hop_sem, ring_sem, later_sem, go_sem, near_sem,
 ):
     z = lax.axis_index("outer")
     c = lax.axis_index("inner")
@@ -86,12 +86,12 @@
     later = [(True, block + 1), (True, block + 2), (c == 0, block + 3)]
     reached = [(near & (n >= 1), n) for near, n in earlier] + [(near & (n < blocks), n) for near, n in later]
     heard = [near & (n >= 0) for near, n in earlier] + [near & (n < blocks) & (block > 0) for near, n in later]
-    near_heads = [row_head(d) for d in range(1, x_chips)] + [column_head(d) for d in (1, y_chips - 1, 2, y_chips - 2)]
+    near_heads = [row_head(1), row_head(x_chips - 1), column_head(1), column_head(y_chips - 1)]
     for condition, n in reached:
         signal_if(condition, barrier, (*place(n), h))
     for head in near_heads:
         signal(barrier, (z, c, head))
-    far_heads = [column_head(d) for d in range(3, y_chips - 2)]
+    far_heads = [row_head(d) for d in range(2, x_chips - 1)] + [column_head(d) for d in range(2, y_chips - 1)]
     for head in far_heads:
         signal_if(first, barrier, (z, c, head))
     for copy in loads[3:]:
@@ -170,10 +170,8 @@
 
     send_near(state, states, state_send, state_recv)
     send_far(state, states, state_send, state_recv, c == 0)
-    for d in (2, y_chips - 2):
-        signal_if(block > 0, ring_sem, (z, c, column_head(d)))
-    for j in range(1, REACH + 1):
-        signal_if((block >= j) & ((c == 1) if j == REACH else True), later_sem, (*place(block - j), h))
+    for head in near_heads:
+        signal_if(block > 0, near_sem, (z, c, head))
 
     loads[3].wait()
     at_t = lax.broadcasted_iota(jnp.int32, (tokens, tokens), 0)
@@ -187,10 +185,17 @@
     for i, cols in enumerate(head_cols):
         gates[:, cols] = jax.nn.sigmoid(g[:, cols].astype(F32)) * gain[i : i + 1].astype(F32)
 
-    pl.when(((c == 0) & (z >= 2)) | ((c == 1) & (z + 2 < groups)))(lambda: pl.semaphore_wait(hop_sem, 1))
+    pl.when(block > 0)(lambda: pl.semaphore_wait(near_sem, len(near_heads)))
+    for d in (2, y_chips - 2):
+        signal_if(block > 0, ring_sem, (z, c, column_head(d)))
+    for j in range(1, REACH + 1):
+        signal_if((block >= j) & ((c == 1) if j == REACH else True), later_sem, (*place(block - j), h))
+
+    pl.when((c == 1) & (z + 2 < groups))(lambda: pl.semaphore_wait(hop_sem, 1))
     send_far(state, states, state_send, state_recv, c == 1)
+    gather(states, state_send, state_recv)
+    pl.when((c == 0) & (z >= 2))(lambda: pl.semaphore_wait(hop_sem, 1))
     signal_if((c == 0) & (z >= 2), later_sem, (z - 2, 1, h))
-    gather(states, state_send, state_recv)
     gathered(states, state_recv)
     loads[6].wait()
     spread(sk, keys, key_send, key_recv)
@@ -311,7 +316,7 @@
             dma((8,)),
             dma((3,)), dma((REACH,)), dma((3,)), dma((REACH,)), dma((3,)), dma((REACH,)),
             dma, dma, dma((REACH + 1,)), dma((REACH + 1,)),
-            regular, regular, regular, regular,
+            regular, regular, regular, regular, regular,
         ],
         compiler_params=pltpu.CompilerParams(collective_id=0, has_side_effects=True),
     )(q, k, v, g, gain, seg, sq, sk)

time: 22.6 us -> 22.6 us (level)
  the two profiles are of different devices: /device:TPU:641 before, /device:TPU:576 now
where the time goes in v7:
time: 22.6 us; the launch traced here: 22.4 us
  Pallas kernels  21.1 us (93%)
  local copies, waits for them, and re-layouts  0.66 us (3%)
  between operations  0.64 us (3%)
    pallas_call x1, Pallas kernels, per_device(): pl.pallas_call(functools.partial(kernel, groups, x_chips, y_chips, total_...  21.1 us
    squeeze x1, local copies, waits for them, and re-layouts, per_device(): return (outs[0], outs[1])  0.66 us

profile of v7, /device:TPU:576, one launch (start us, length us, event | category | flops | bytes accessed | tf_op | source)
XLA Modules:
  0.0 22.4 jit_solution(2856409179807711446)
XLA Ops:
  0.6 21.1 %shard_map.95 = bf16[2,128,256]{2,1,0:T(8,128)(2,1)S(1)} custom-call(bf16[128,256]{1,0:T(8,128)(2,1)} %q_in.1, bf16[128,256]{1,0:T(8,128)(2,1)} %k_in.1, bf16[128,256]{1,0:T(8,128)(2,1)} %v_in.1, bf16[128,256]{1,0:T(8,128)(2,1)} %g_in.1, bf16[2,128]{1,0:T(2,128)(2,1)} %bitcast.6, s32[1,128]{1,0:T(1,128)} %bitcast.7, bf16[128,256]{1,0:T(8,128)(2,1)} %sq_in.1, ...), custom_call_target="tpu_custom_call" | custom-call | tf_op jit(solution)/shard_map/pallas_call | solution.py:299
  21.8 0.7 %slice_bitcast_fusion = (bf16[128,256]{1,0:T(8,128)(2,1)}, bf16[128,256]{1,0:T(8,128)(2,1)}) fusion(bf16[2,128,256]{2,1,0:T(8,128)(2,1)S(1)} %shard_map.95), kind=kLoop, calls=%fused_computation | loop fusion | bytes 262144 | tf_op jit(solution)/shard_map/squeeze | solution.py:323

commit v8 on v5

--- a/solution.py
+++ b/solution.py
@@ -196,11 +196,10 @@
     spread(sk, keys, key_send, key_recv)
     doc_rows = [states[j, columns : columns + 1, :].astype(F32) for j in range(REACH)]
     for cols in head_cols:
-        q_f32 = q[:, cols].astype(F32)
         carried = None
         for j in range(REACH):
             last = doc_rows[j][:, tokens - 1 :]
-            part = matmul(jnp.where(doc_col == last, q_f32, 0.0).astype(BF16), states[j, cols, :])
+            part = jnp.where(doc_col == last, matmul(q[:, cols], states[j, cols, :]), 0.0)
             carried = part if carried is None else carried + part
         mixed[:, cols] += carried
 
@@ -209,7 +208,7 @@
 
     pl.when(block > 0)(lambda: pl.semaphore_wait(ring_sem, 2))
     pl.when(first)(lambda: pl.semaphore_wait(barrier, len(near_heads) + len(far_heads)))
-    for d in range(1, y_chips):
+    for d in sorted(range(1, y_chips), key=lambda d: abs(d - y_chips // 2)):
         remote(own_row, rows_y.at[y], y_send, y_recv, (z, c, column_head(d))).start()
     rows_y[y] = own_row[...]
     mid[...] = (mixed[...] * gates[...]).astype(BF16)
@@ -226,7 +225,7 @@
 
         @pl.when(block + j < blocks)
         def _(j=j):
-            for d in range(0 if j else 1, x_chips):
+            for d in (2, 1, 3) + ((0,) if j else ()):
                 device = (*place(block + j), row_head(d))
                 remote(column_row, rows_x.at[j, x], x_send.at[j], x_recv.at[j], device).start()
 

time: 22.8 us -> 22.7 us (level)
  no operation moved by 1% of the time
where the time goes in v8:
time: 22.7 us; the launch traced here: 22.6 us
  Pallas kernels  21.3 us (94%)
  local copies, waits for them, and re-layouts  0.66 us (3%)
  between operations  0.64 us (3%)
    pallas_call x1, Pallas kernels, per_device(): pl.pallas_call(functools.partial(kernel, groups, x_chips, y_chips, total_...  21.3 us
    squeeze x1, local copies, waits for them, and re-layouts, per_device(): return (outs[0], outs[1])  0.66 us

profile of v8, /device:TPU:576, one launch (start us, length us, event | category | flops | bytes accessed | tf_op | source)
XLA Modules:
  0.0 22.6 jit_solution(8707466566190218198)
XLA Ops:
  0.6 21.3 %shard_map.95 = bf16[2,128,256]{2,1,0:T(8,128)(2,1)S(1)} custom-call(bf16[128,256]{1,0:T(8,128)(2,1)} %q_in.1, bf16[128,256]{1,0:T(8,128)(2,1)} %k_in.1, bf16[128,256]{1,0:T(8,128)(2,1)} %v_in.1, bf16[128,256]{1,0:T(8,128)(2,1)} %g_in.1, bf16[2,128]{1,0:T(2,128)(2,1)} %bitcast.6, s32[1,128]{1,0:T(1,128)} %bitcast.7, bf16[128,256]{1,0:T(8,128)(2,1)} %sq_in.1, ...), custom_call_target="tpu_custom_call" | custom-call | tf_op jit(solution)/shard_map/pallas_call | solution.py:294
  21.9 0.7 %slice_bitcast_fusion = (bf16[128,256]{1,0:T(8,128)(2,1)}, bf16[128,256]{1,0:T(8,128)(2,1)}) fusion(bf16[2,128,256]{2,1,0:T(8,128)(2,1)S(1)} %shard_map.95), kind=kLoop, calls=%fused_computation | loop fusion | bytes 262144 | tf_op jit(solution)/shard_map/squeeze | solution.py:318
